TPU v7x, 32 devices: a whole 2x2x4 slice. The times are simulated.
32 devices in a mesh: replica: 16 (over z, x, core), shard: 2 (over y).
Axes of the slice: x: 2, y: 2, z: 4, core: 2. Of those that a mesh axis runs over, the one named last changes fastest.
Arguments:
- latents: bfloat16 [32, 1024, 1152], P('replica', 'shard'), may hold values from -6 to 6
- conditions: bfloat16 [32, 1152], P('replica'), may hold values from -6 to 6
- cotangent: bfloat16 [32, 1024, 1152], P('replica', 'shard'), may hold values from -6 to 6
- counts: int32 [16], P('replica'), may hold values from 1 to 2, as said below
- w_ada: bfloat16 [1152, 6912], P('shard'), may hold values from -0.1875 to 0.1875
- b_ada: bfloat16 [6912], P('shard'), may hold values from -3 to 3
- w_qkv: bfloat16 [1152, 3456], P('shard'), may hold values from -0.1875 to 0.1875
- b_qv: bfloat16 [2304], P('shard'), may hold values from -3 to 3
- w_proj: bfloat16 [1152, 1152], P('shard'), may hold values from -3.5 to 3.5
- b_proj: bfloat16 [1152], P('shard'), may hold values from -3 to 3
- w_fc1: bfloat16 [1152, 4608], P('shard'), may hold values from -0.1875 to 0.1875
- b_fc1: bfloat16 [4608], P('shard'), may hold values from -3 to 3
- w_fc2: bfloat16 [4608, 1152], P('shard'), may hold values from -0.09375 to 0.09375
- b_fc2: bfloat16 [1152], P('shard'), may hold values from -3 to 3
Outputs:
- output: bfloat16 [32, 1024, 1152], P('replica', 'shard')
- grad_latents: float32 [32, 1024, 1152], P('replica', 'shard')
- grad_conditions: float32 [32, 1152], P('replica')
- grad_w_ada: float32 [1152, 6912], P('shard')
- grad_b_ada: float32 [6912], P('shard')
- grad_w_qkv: float32 [1152, 3456], P('shard')
- grad_b_qv: float32 [2304], P('shard')
- grad_w_proj: float32 [1152, 1152], P('shard')
- grad_b_proj: float32 [1152], P('shard')
- grad_w_fc1: float32 [1152, 4608], P('shard')
- grad_b_fc1: float32 [4608], P('shard')
- grad_w_fc2: float32 [4608, 1152], P('shard')
- grad_b_fc2: float32 [1152], P('shard')
Inputs may be any that keep to these rules, and one draw needn't show every extreme that they name: counts[r] live slots on replica r are its slots 0 to counts[r] - 1 of 2; some replica has all 2 live.
All inputs are finite; a program needn't handle non-finite values.
Results may differ from a plain program's by a relative error of at most 0.019.
Values may be sent and summed in bfloat16 or wider, within the bound.
A program may use at most 512 MiB of HBM per device.

v0:
```python
from functools import partial
import math

import jax
import jax.numpy as jnp
from jax import lax
from jax.sharding import PartitionSpec as P

HEADS = 16
HDIM = 72


epsilon = 1e-06


def layer_stats(values):
    centered = values - jnp.mean(values, axis=-1, keepdims=True)
    inverse = lax.rsqrt(jnp.mean(centered * centered, axis=-1, keepdims=True) + epsilon)
    return (centered * inverse, inverse)


def layer_back(normal, inverse, d_normal):
    first_mean = jnp.mean(d_normal, axis=-1, keepdims=True)
    second_mean = jnp.mean(d_normal * normal, axis=-1, keepdims=True)
    return inverse * (d_normal - first_mean - normal * second_mean)


def contract_last(left, right):
    return lax.dot_general(
        left, right, (((1,), (1,)), ((), ())), preferred_element_type=jnp.float32
    )


def forward_product(inputs, whole_pair):
    return (
        jnp.dot(inputs, whole_pair[0], preferred_element_type=jnp.float32),
        whole_pair[1].astype(jnp.float32),
    )


def backward_product(grads, whole_pair):
    return contract_last(grads, whole_pair[0])


def owner_grads(inputs, grads, weight_rows, bias_terms):
    columns = lax.slice_in_dim(inputs, 0, weight_rows * lax.axis_size("shard"), axis=1)
    weight_grad = lax.psum_scatter(
        lax.dot_general(
            columns, grads, (((0,), (0,)), ((), ())), preferred_element_type=jnp.float32
        ).astype(jnp.bfloat16),
        "shard",
        scatter_dimension=0,
        tiled=True,
    ).astype(jnp.float32)
    bias_grad = lax.psum_scatter(
        bias_terms.astype(jnp.bfloat16), "shard", scatter_dimension=0, tiled=True
    ).astype(jnp.float32)
    return (weight_grad, bias_grad)


def shards(
    latents,
    conditions,
    cotangent,
    counts,
    w_ada,
    b_ada,
    w_qkv,
    b_qv,
    w_proj,
    b_proj,
    w_fc1,
    b_fc1,
    w_fc2,
    b_fc2,
):
    slots, block, width = latents.shape
    n_rows = slots * block
    scale = 1.0 / math.sqrt(HDIM)
    live = (jnp.arange(slots, dtype=jnp.int32) < counts[0]).astype(jnp.float32)[:, None, None]
    gathered = (
        lax.all_gather(w_ada, "shard", axis=0, tiled=True),
        lax.all_gather(b_ada, "shard", axis=0, tiled=True),
        lax.all_gather(w_qkv, "shard", axis=0, tiled=True),
        lax.all_gather(b_qv, "shard", axis=0, tiled=True),
        lax.all_gather(w_proj, "shard", axis=0, tiled=True),
        lax.all_gather(b_proj, "shard", axis=0, tiled=True),
        lax.all_gather(w_fc1, "shard", axis=0, tiled=True),
        lax.all_gather(b_fc1, "shard", axis=0, tiled=True),
        lax.all_gather(w_fc2, "shard", axis=0, tiled=True),
        lax.all_gather(b_fc2, "shard", axis=0, tiled=True),
    )
    full_ada = (gathered[0], gathered[1])
    full_qkv = (gathered[2], gathered[3])
    full_proj = (gathered[4], gathered[5])
    full_fc1 = (gathered[6], gathered[7])
    full_fc2 = (gathered[8], gathered[9])
    cond_float = conditions.astype(jnp.float32)
    cond_act = jax.nn.silu(cond_float).astype(jnp.bfloat16)
    ada_prod, ada_bias = forward_product(cond_act, full_ada)
    modul = ada_prod + ada_bias
    shift_a, scale_a, gate_a, shift_m, scale_m, gate_m = [
        piece[:, None, :] for piece in jnp.split(modul, 6, axis=1)
    ]
    tokens = latents.astype(jnp.float32)
    norm_a, inv_a = layer_stats(tokens)
    normed = (norm_a * (1.0 + scale_a) + shift_a).astype(jnp.bfloat16).reshape(n_rows, width)
    qkv_prod, qv_bias = forward_product(normed, full_qkv)
    query = (
        (qkv_prod[:, :width] + qv_bias[:width])
        .astype(jnp.bfloat16)
        .reshape(slots, block, HEADS, HDIM)
    )
    keys_own = qkv_prod[:, width : 2 * width].astype(jnp.bfloat16).reshape(slots, block, width)
    values_own = (
        (qkv_prod[:, 2 * width :] + qv_bias[width:])
        .astype(jnp.bfloat16)
        .reshape(slots, block, width)
    )
    keys_all, values_all = (
        lax.all_gather(keys_own, "shard", axis=1, tiled=True),
        lax.all_gather(values_own, "shard", axis=1, tiled=True),
    )
    length = keys_all.shape[1]
    keys_h = keys_all.reshape(slots, length, HEADS, HDIM)
    values_h = values_all.reshape(slots, length, HEADS, HDIM)
    scores = (
        jnp.einsum("sqhd,skhd->shqk", query, keys_h, preferred_element_type=jnp.float32) * scale
    )
    top_score = jnp.max(scores, axis=-1, keepdims=True)
    log_total = top_score + jnp.log(jnp.sum(jnp.exp(scores - top_score), axis=-1, keepdims=True))
    probs_low = jnp.exp(scores - log_total).astype(jnp.bfloat16)
    attended = jnp.einsum(
        "shqk,skhd->sqhd", probs_low, values_h, preferred_element_type=jnp.float32
    )
    attended = attended.astype(jnp.bfloat16).reshape(n_rows, width)
    proj_prod, proj_bias = forward_product(attended, full_proj)
    branch_a = (proj_prod + proj_bias).reshape(slots, block, width)
    resid = tokens + gate_a * branch_a
    norm_m, inv_m = layer_stats(resid)
    mixed = (norm_m * (1.0 + scale_m) + shift_m).astype(jnp.bfloat16).reshape(n_rows, width)
    fc1_prod, fc1_bias = forward_product(mixed, full_fc1)
    activated, gelu_back = jax.vjp(partial(jax.nn.gelu, approximate=True), fc1_prod + fc1_bias)
    hidden = activated.astype(jnp.bfloat16)
    fc2_prod, fc2_bias = forward_product(hidden, full_fc2)
    branch_m = (fc2_prod + fc2_bias).reshape(slots, block, width)
    final = resid + gate_m * branch_m
    output = (final * live).astype(jnp.bfloat16)
    d_out = cotangent.astype(jnp.float32) * live
    d_gate_m = jnp.sum(d_out * branch_m, axis=1)
    d_branch_m = (gate_m * d_out).astype(jnp.bfloat16).reshape(n_rows, width)
    pair_fc2 = owner_grads(
        hidden, d_branch_m, w_fc2.shape[0], jnp.sum(d_branch_m, axis=0, dtype=jnp.float32)
    )
    d_hidden = backward_product(d_branch_m, full_fc2)
    d_pre = gelu_back(d_hidden)[0].astype(jnp.bfloat16)
    pair_fc1 = owner_grads(mixed, d_pre, w_fc1.shape[0], jnp.sum(d_pre, axis=0, dtype=jnp.float32))
    d_mixed = backward_product(d_pre, full_fc1).reshape(slots, block, width)
    d_shift_m = jnp.sum(d_mixed, axis=1)
    d_scale_m = jnp.sum(d_mixed * norm_m, axis=1)
    d_resid = d_out + layer_back(norm_m, inv_m, d_mixed * (1.0 + scale_m))
    d_gate_a = jnp.sum(d_resid * branch_a, axis=1)
    d_branch_a = (gate_a * d_resid).astype(jnp.bfloat16).reshape(n_rows, width)
    pair_proj = owner_grads(
        attended, d_branch_a, w_proj.shape[0], jnp.sum(d_branch_a, axis=0, dtype=jnp.float32)
    )
    d_attended = (
        backward_product(d_branch_a, full_proj)
        .astype(jnp.bfloat16)
        .reshape(slots, block, HEADS, HDIM)
    )
    scores = (
        jnp.einsum("sqhd,skhd->shqk", query, keys_h, preferred_element_type=jnp.float32) * scale
    )
    probs = jnp.exp(scores - log_total)
    d_probs = jnp.einsum(
        "sqhd,skhd->shqk", d_attended, values_h, preferred_element_type=jnp.float32
    )
    inner = jnp.sum(d_probs * probs, axis=-1, keepdims=True)
    d_scores = (probs * (d_probs - inner)).astype(jnp.bfloat16)
    d_query = (
        (
            jnp.einsum("shqk,skhd->sqhd", d_scores, keys_h, preferred_element_type=jnp.float32)
            * scale
        )
        .astype(jnp.bfloat16)
        .reshape(n_rows, width)
    )
    key_terms = (
        jnp.einsum("shqk,sqhd->skhd", d_scores, query, preferred_element_type=jnp.float32).reshape(
            slots, length, width
        )
        * scale
    )
    value_terms = jnp.einsum(
        "shqk,sqhd->skhd",
        probs.astype(jnp.bfloat16),
        d_attended,
        preferred_element_type=jnp.float32,
    ).reshape(slots, length, width)
    d_keys, d_values = (
        lax.psum_scatter(
            key_terms.astype(jnp.bfloat16), "shard", scatter_dimension=1, tiled=True
        ).astype(jnp.float32),
        lax.psum_scatter(
            value_terms.astype(jnp.bfloat16), "shard", scatter_dimension=1, tiled=True
        ).astype(jnp.float32),
    )
    d_keys = d_keys.astype(jnp.bfloat16).reshape(n_rows, width)
    d_values = d_values.astype(jnp.bfloat16).reshape(n_rows, width)
    d_qkv = jnp.concatenate([d_query, d_keys, d_values], axis=1)
    qv_terms = jnp.concatenate(
        [jnp.sum(d_query, axis=0, dtype=jnp.float32), jnp.sum(d_values, axis=0, dtype=jnp.float32)]
    )
    pair_qkv = owner_grads(normed, d_qkv, w_qkv.shape[0], qv_terms)
    d_normed = backward_product(d_qkv, full_qkv).reshape(slots, block, width)
    d_shift_a = jnp.sum(d_normed, axis=1)
    d_scale_a = jnp.sum(d_normed * norm_a, axis=1)
    grad_latents = d_resid + layer_back(norm_a, inv_a, d_normed * (1.0 + scale_a))
    d_modul_part = jnp.concatenate(
        [d_shift_a, d_scale_a, d_gate_a, d_shift_m, d_scale_m, d_gate_m], axis=1
    )
    d_modul = lax.psum(d_modul_part.astype(jnp.bfloat16), "shard")
    index = lax.axis_index("shard")
    ada_rows = w_ada.shape[0]
    ada_length = b_ada.shape[0]
    own_cond = lax.dynamic_slice_in_dim(cond_act, index * ada_rows, ada_rows, 1)
    grad_w_ada = lax.dot_general(
        own_cond, d_modul, (((0,), (0,)), ((), ())), preferred_element_type=jnp.float32
    )
    grad_b_ada = lax.dynamic_slice_in_dim(
        jnp.sum(d_modul, axis=0, dtype=jnp.float32), index * ada_length, ada_length, 0
    )
    pair_ada = (grad_w_ada, grad_b_ada)
    d_cond_act = backward_product(d_modul, full_ada)
    _, silu_back = jax.vjp(jax.nn.silu, cond_float)
    grad_conditions = silu_back(d_cond_act)[0]
    summed = (
        lax.psum(pair_ada[0].astype(jnp.bfloat16), "replica").astype(jnp.float32),
        lax.psum(pair_ada[1].astype(jnp.bfloat16), "replica").astype(jnp.float32),
        lax.psum(pair_qkv[0].astype(jnp.bfloat16), "replica").astype(jnp.float32),
        lax.psum(pair_qkv[1].astype(jnp.bfloat16), "replica").astype(jnp.float32),
        lax.psum(pair_proj[0].astype(jnp.bfloat16), "replica").astype(jnp.float32),
        lax.psum(pair_proj[1].astype(jnp.bfloat16), "replica").astype(jnp.float32),
        lax.psum(pair_fc1[0].astype(jnp.bfloat16), "replica").astype(jnp.float32),
        lax.psum(pair_fc1[1].astype(jnp.bfloat16), "replica").astype(jnp.float32),
        lax.psum(pair_fc2[0].astype(jnp.bfloat16), "replica").astype(jnp.float32),
        lax.psum(pair_fc2[1].astype(jnp.bfloat16), "replica").astype(jnp.float32),
    )
    pair_ada = (summed[0], summed[1])
    pair_qkv = (summed[2], summed[3])
    pair_proj = (summed[4], summed[5])
    pair_fc1 = (summed[6], summed[7])
    pair_fc2 = (summed[8], summed[9])
    return (
        output,
        grad_latents,
        grad_conditions,
        pair_ada[0],
        pair_ada[1],
        pair_qkv[0],
        pair_qkv[1],
        pair_proj[0],
        pair_proj[1],
        pair_fc1[0],
        pair_fc1[1],
        pair_fc2[0],
        pair_fc2[1],
    )


def solution(mesh):
    placed = (
        P("replica", "shard", None),
        P("replica", None),
        P("replica", "shard", None),
        P("replica"),
        P("shard", None),
        P("shard"),
        P("shard", None),
        P("shard"),
        P("shard", None),
        P("shard"),
        P("shard", None),
        P("shard"),
        P("shard", None),
        P("shard"),
    )
    return jax.shard_map(
        shards,
        mesh=mesh,
        in_specs=placed,
        out_specs=(
            P("replica", "shard", None),
            P("replica", "shard", None),
            P("replica", None),
            P("shard", None),
            P("shard"),
            P("shard", None),
            P("shard"),
            P("shard", None),
            P("shard"),
            P("shard", None),
            P("shard"),
            P("shard", None),
            P("shard"),
        ),
        check_vma=False,
    )
```

profile of v0, /device:TPU:0, one launch (start us, length us, event | category | flops | bytes accessed | tf_op | source)
XLA Modules:
  0.0 1932.2 jit_solution(709824558595214177)
XLA Ops:
  15.4 186.2 %all-gather.11.cloned.1.call-done = bf16[1152,6912]{1,0:T(8,128)(2,1)} async-done(((bf16[576,6912]{1,0:T(8,128)(2,1)}), bf16[1152,6912]{1,0:T(8,128)(2,1)}) %all-gather.11.cloned.1.call-update) | async-done | bytes 15925264 | tf_op jit(solution)/shard_map/all_gather | solution.py:82
  211.7 90.6 %all-gather.13.cloned.1.call-done = bf16[1152,3456]{1,0:T(8,128)(2,1)} async-done(((bf16[576,3456]{1,0:T(8,128)(2,1)}), bf16[1152,3456]{1,0:T(8,128)(2,1)}) %all-gather.13.cloned.1.call-update) | async-done | bytes 7962640 | tf_op jit(solution)/shard_map/all_gather | solution.py:84
  392.2 27.5 %multiply_reduce_fusion.1 = (f32[2,16,512]{2,1,0:T(8,128)S(1)}, f32[2,16,512,1024]{3,2,1,0:T(8,128)}) fusion(bf16[2,512,16,72]{1,3,2,0:T(8,128)(2,1)} %copy.64, bf16[2,1024,16,72]{1,3,2,0:T(8,128)(2,1)} %bitcast.98), kind=kOutput, calls=%fused_computation.4 | convolution fusion | flops 2449457152 | bytes 74252288 | tf_op jit(solution)/shard_map/sqhd,skhd->shqk/dot_general | solution.py:128
  419.6 21.3 %exponential_reduce_fusion = f32[2,16,512]{2,1,0:T(8,128)S(1)} fusion(f32[2,16,512,1024]{3,2,1,0:T(8,128)} %get-tuple-element.64, f32[2,16,512]{2,1,0:T(8,128)S(1)} %get-tuple-element.63), kind=kLoop, calls=%fused_computation.3 | loop fusion | flops 50315264 | bytes 67239936 | tf_op jit(solution)/shard_map/reduce_sum | solution.py:131
  456.9 27.9 %convert_bitcast_fusion = bf16[2,512,16,72]{1,3,2,0:T(8,128)(2,1)} fusion(bf16[2,1024,16,72]{1,3,2,0:T(8,128)(2,1)} %bitcast.94, f32[2,16,512,1024]{3,2,1,0:T(8,128)} %get-tuple-element.64, f32[2,16,512]{2,1,0:T(8,128)S(1)} %log_add_fusion), kind=kOutput, calls=%fused_computation.74 | convolution fusion | flops 2467430400 | bytes 74252288 | tf_op jit(solution)/shard_map/shqk,skhd->sqhd/dot_general | solution.py:133
  503.3 120.2 %all-gather.21.cloned.1.call-done = bf16[1152,4608]{1,0:T(8,128)(2,1)} async-done(((bf16[576,4608]{1,0:T(8,128)(2,1)}), bf16[1152,4608]{1,0:T(8,128)(2,1)}) %all-gather.21.cloned.1.call-update) | async-done | bytes 10616848 | tf_op jit(solution)/shard_map/all_gather | solution.py:88
  623.4 19.1 fusion.60
  642.5 113.4 %all-gather.23.cloned.1.call-done = bf16[4608,1152]{1,0:T(8,128)(2,1)} async-done(((bf16[2304,1152]{1,0:T(8,128)(2,1)}), bf16[4608,1152]{1,0:T(8,128)(2,1)}) %all-gather.23.cloned.1.call-update) | async-done | bytes 10616848 | tf_op jit(solution)/shard_map/all_gather | solution.py:90
  756.0 30.4 %fusion.52 = (bf16[4608]{0:T(1024)(128)(2,1)}, bf16[1024,4608]{1,0:T(8,128)(2,1)}) fusion(f32[1024,4608]{1,0:T(8,128)} %fusion.60, f32[4608]{0:T(1024)S(1)} %reshape.203, bf16[1024,1152]{1,0:T(8,128)(2,1)} %bitcast.118, bf16[4608,1152]{1,0:T(8,128)(2,1)} %all-gather.23.cloned.1.call-done), kind=kOutput, calls=%fused_computation.117 | convolution fusion | flops 10975440896 | bytes 41315328 | tf_op jit(solution)/shard_map/dot_general | solution.py:29
  786.3 19.9 %fusion.29 = (f32[1024]{0:T(1024)S(1)}, f32[1024,1152]{1,0:T(8,128)}) fusion(f32[2,1152]{1,0:T(2,128)S(1)} %get-tuple-element.54, bf16[1024,4608]{1,0:T(8,128)(2,1)} %get-tuple-element.41, bf16[1152,4608]{1,0:T(8,128)(2,1)} %all-gather.21.cloned.1.call-done), kind=kOutput, calls=%fused_computation.53 | convolution fusion | flops 10873994240 | bytes 24785920 | tf_op jit(solution)/shard_map/dot_general | solution.py:29
  806.3 20.9 %convolution_add_fusion.1 = f32[1024,1152]{1,0:T(8,128)S(1)} fusion(bf16[4608,1152]{1,0:T(8,128)(2,1)} %all-gather.23.cloned.1.call-done, f32[1152]{0:T(1024)S(1)} %copy-done.40, f32[1024,4608]{1,0:T(8,128)} %fusion.60, f32[4608]{0:T(1024)S(1)} %reshape.203), kind=kOutput, calls=%fused_computation.35 | convolution fusion | flops 10920001536 | bytes 34232832 | tf_op jit(solution)/shard_map/dot_general | solution.py:36
  856.2 26.0 %fusion.32 = bf16[2,16,72,1024]{3,2,1,0:T(8,128)(2,1)} fusion(bf16[2,512,16,72]{1,3,2,0:T(8,128)(2,1)S(1)} %copy.67, f32[2,16,512,1024]{3,2,1,0:T(8,128)} %get-tuple-element.64, f32[2,16,512]{2,1,0:T(8,128)S(1)} %copy-done.10), kind=kOutput, calls=%fused_computation.72 | convolution fusion | flops 2468610048 | bytes 74252288 | tf_op jit(solution)/shard_map/shqk,sqhd->skhd/dot_general | solution.py:195
  889.0 49.1 %multiply_reduce_fusion = (f32[2,16,512]{2,1,0:T(8,128)S(1)}, f32[2,16,512,1024]{3,2,1,0:T(8,128)}) fusion(f32[2,16,512,1024]{3,2,1,0:T(8,128)} %get-tuple-element.64, f32[2,16,512]{2,1,0:T(8,128)S(1)} %copy-done.10, bf16[2,512,16,72]{1,3,2,0:T(8,128)(2,1)S(1)} %copy.67, bf16[2,1024,16,72]{1,3,2,0:T(8,128)(2,1)} %bitcast.95), kind=kOutput, calls=%fused_computation.1 | convolution fusion | flops 2483011584 | bytes 141426688 | tf_op jit(solution)/shard_map/sqhd,skhd->shqk/dot_general | solution.py:176
  938.2 53.3 %multiply_convert_fusion = bf16[2,16,512,1024]{3,2,1,0:T(8,128)(2,1)} fusion(f32[2,16,512,1024]{3,2,1,0:T(8,128)} %get-tuple-element.68, f32[2,16,512,1024]{3,2,1,0:T(8,128)} %get-tuple-element.64, f32[2,16,512]{2,1,0:T(8,128)S(1)} %get-tuple-element.67, f32[2,16,512]{2,1,0:T(8,128)S(1)} %copy-done.10), kind=kLoop, calls=%fused_computation | loop fusion | flops 83886080 | bytes 167903232 | tf_op jit(solution)/shard_map/convert_element_type | solution.py:180
  991.5 18.7 multiply_convert_fusion.2
  1025.0 23.4 %convolution_convert_fusion = bf16[4608,1152]{1,0:T(8,128)(2,1)} fusion(bf16[1024,1152]{1,0:T(8,128)(2,1)} %bitcast.119, f32[1024,4608]{1,0:T(8,128)} %fusion.60, f32[4608]{0:T(1024)S(1)} %copy-done.33), kind=kOutput, calls=%fused_computation.8 | convolution fusion | flops 10924130304 | bytes 31868928 | tf_op jit(solution)/shard_map/dot_general | solution.py:48
  1050.1 17.4 convolution_convert_fusion.1
  1067.7 18.1 fusion.58
  1113.1 16.0 fusion.28
  1168.5 76.7 %reduce-scatter.17.cloned.1.call-done = bf16[2304,1152]{1,0:T(8,128)(2,1)} async-done(((bf16[4608,1152]{1,0:T(8,128)(2,1)}), bf16[2304,1152]{1,0:T(8,128)(2,1)}) %reduce-scatter.17.cloned.1.call-update) | async-done | bytes 5308432 | tf_op jit(solution)/shard_map/reduce_scatter | solution.py:47
  1245.2 126.1 %reduce-scatter.15.cloned.1.call-done = bf16[576,4608]{1,0:T(8,128)(2,1)} async-done(((bf16[1152,4608]{1,0:T(8,128)(2,1)}), bf16[576,4608]{1,0:T(8,128)(2,1)}) %reduce-scatter.15.cloned.1.call-update) | async-done | bytes 5308432 | tf_op jit(solution)/shard_map/reduce_scatter | solution.py:47
  1371.4 97.6 %reduce-scatter.11.cloned.1.call-done = bf16[576,3456]{1,0:T(8,128)(2,1)} async-done(((bf16[1152,3456]{1,0:T(8,128)(2,1)}), bf16[576,3456]{1,0:T(8,128)(2,1)}) %reduce-scatter.11.cloned.1.call-update) | async-done | bytes 3981328 | tf_op jit(solution)/shard_map/reduce_scatter | solution.py:47
  1471.5 64.6 %all-reduce.6 = (bf16[3456]{0:T(1024)(128)(2,1)S(1)}, bf16[1152]{0:T(1024)(128)(2,1)S(1)}, bf16[576]{0:T(1024)(128)(2,1)S(1)}, bf16[2304]{0:T(1024)(128)(2,1)S(1)}, bf16[576]{0:T(1024)(128)(2,1)S(1)}) all-reduce(bf16[3456]{0:T(1024)(128)(2,1)S(1)} %dynamic_slice.11, ...), channel_id=1, replica_groups=mesh['replica'=16,'shard'=2] {'replica'}, use_global_device_ids=true, to_apply=%region_22.23 | all-reduce | flops 8064 | bytes 32256 | tf_op jit(solution)/shard_map/psum | solution.py:240
  1539.1 356.0 %all-reduce.12.cloned.1.call-done = (bf16[576,6912]{1,0:T(8,128)(2,1)}, bf16[576,3456]{1,0:T(8,128)(2,1)}, bf16[576,1152]{1,0:T(8,128)(2,1)}, bf16[576,4608]{1,0:T(8,128)(2,1)}, bf16[2304,1152]{1,0:T(8,128)(2,1)}) async-done(((bf16[576,6912]{1,0:T(8,128)(2,1)}, bf16[576,3456]{1,0:T(8,128)(2,1)}, bf16[576,1152]{1,0:T(8,128)(2,1)}, bf16[576,4608]{1,0:T(8,128)(2,1)}, bf16[2304,1152]{1,0:T(8,128)(2,1)}), ...) | async-done | bytes 23887888 | tf_op jit(solution)/shard_map/psum | solution.py:239
  (243 shorter events, 293.1 us)
Async XLA Ops:
  7.2 194.4 %all-gather.11.cloned.1.call-start = ((), (), s32[]{:S(2)}) async-start(), calls=%async_computation.6 | async-start | bytes 23887872 | tf_op jit(solution)/shard_map/all_gather | solution.py:82
  7.9 193.7 %copy-start.30 = (bf16[2,1152]{1,0:T(2,128)(2,1)S(1)}, bf16[2,1152]{1,0:T(2,128)(2,1)}, u32[]{:S(2)}) copy-start(bf16[2,1152]{1,0:T(2,128)(2,1)} %param.15) | copy-start | bytes 13828
  7.9 294.4 %all-gather.13.cloned.1.call-start = ((), (), s32[]{:S(2)}) async-start(), calls=%async_computation.7 | async-start | bytes 11943936 | tf_op jit(solution)/shard_map/all_gather | solution.py:84
  8.7 376.9 %all-gather.17.cloned.1.call-start = ((), (), s32[]{:S(2)}) async-start(), calls=%async_computation.9 | async-start | bytes 7077888 | tf_op jit(solution)/shard_map/all_gather | solution.py:121
  14.6 194.7 %copy-start.20 = (f32[2,512]{1,0:T(2,128)}, f32[2,512]{1,0:T(2,128)S(1)}, u32[]{:S(2)}) copy-start(f32[2,512]{1,0:T(2,128)S(1)} %broadcast_multiply_fusion.5) | copy-start | bytes 12292
  15.4 193.9 %copy-start.28 = (f32[2,512]{1,0:T(2,128)}, f32[2,512]{1,0:T(2,128)S(1)}, u32[]{:S(2)}) copy-start(f32[2,512]{1,0:T(2,128)S(1)} %add_rsqrt_fusion.1) | copy-start | bytes 12292
  209.3 106.1 %copy-start.16 = (f32[2,1152]{1,0:T(2,128)}, f32[2,1152]{1,0:T(2,128)S(1)}, u32[]{:S(2)}) copy-start(f32[2,1152]{1,0:T(2,128)S(1)} %get-tuple-element.56) | copy-start | bytes 27652
  209.3 157.2 %copy-start.24 = (f32[2,1152]{1,0:T(2,128)}, f32[2,1152]{1,0:T(2,128)S(1)}, u32[]{:S(2)}) copy-start(f32[2,1152]{1,0:T(2,128)S(1)} %get-tuple-element.52) | copy-start | bytes 27652
  209.3 287.8 %copy-start.22 = (f32[2,1152]{1,0:T(2,128)}, f32[2,1152]{1,0:T(2,128)S(1)}, u32[]{:S(2)}) copy-start(f32[2,1152]{1,0:T(2,128)S(1)} %get-tuple-element.57) | copy-start | bytes 27652
  322.4 127.8 %all-gather.15.cloned.1.call-start = ((), (), s32[]{:S(2)}) async-start(), calls=%async_computation.8 | async-start | bytes 7077888 | tf_op jit(solution)/shard_map/all_gather | solution.py:122
  334.7 156.4 %all-gather.19.cloned.1.call-start = ((), (), s32[]{:S(2)}) async-start(), calls=%async_computation.10 | async-start | bytes 3981312 | tf_op jit(solution)/shard_map/all_gather | solution.py:86
  335.3 288.1 %all-gather.21.cloned.1.call-start = ((), (), s32[]{:S(2)}) async-start(), calls=%async_computation.11 | async-start | bytes 15925248 | tf_op jit(solution)/shard_map/all_gather | solution.py:88
  335.9 420.1 %all-gather.23.cloned.1.call-start = ((), (), s32[]{:S(2)}) async-start(), calls=%async_computation.12 | async-start | bytes 15925248 | tf_op jit(solution)/shard_map/all_gather | solution.py:90
  336.6 753.6 %reduce-scatter.9.cloned.1.call-start = ((), (), s32[]{:S(2)}) async-start(), calls=%async_computation.14 | async-start | bytes 7077888 | tf_op jit(solution)/shard_map/reduce_scatter | solution.py:205
  349.8 456.5 %copy-start.32 = (f32[4608]{0:T(1024)}, f32[4608]{0:T(1024)S(1)}, u32[]{:S(2)}) copy-start(f32[4608]{0:T(1024)S(1)} %reshape.203) | copy-start | bytes 55300
  500.2 142.3 %copy-start.26 = (f32[2,512]{1,0:T(2,128)}, f32[2,512]{1,0:T(2,128)S(1)}, u32[]{:S(2)}) copy-start(f32[2,512]{1,0:T(2,128)S(1)} %add_rsqrt_fusion) | copy-start | bytes 12292
  503.3 139.3 %copy-start.13 = (bf16[2,512,1152]{2,1,0:T(8,128)(2,1)}, bf16[2,512,1152]{2,1,0:T(8,128)(2,1)S(1)}, u32[]{:S(2)}) copy-start(bf16[2,512,1152]{2,1,0:T(8,128)(2,1)S(1)} %add_convert_fusion) | copy-start | bytes 7077892
  889.0 205.6 %reduce-scatter.7.cloned.1.call-start = ((), (), s32[]{:S(2)}) async-start(), calls=%async_computation.13 | async-start | bytes 7077888 | tf_op jit(solution)/shard_map/reduce_scatter | solution.py:202
  938.2 53.3 %copy-start.5 = (bf16[2,512,16,72]{1,3,2,0:T(8,128)(2,1)S(1)}, bf16[2,512,16,72]{1,3,2,0:T(8,128)(2,1)}, u32[]{:S(2)}) copy-start(bf16[2,512,16,72]{1,3,2,0:T(8,128)(2,1)} %copy.64) | copy-start | bytes 7077892
  1016.9 151.6 %reduce-scatter.13.cloned.1.call-start = ((), (), s32[]{:S(2)}) async-start(), calls=%async_computation.16 | async-start | bytes 3981312 | tf_op jit(solution)/shard_map/reduce_scatter | solution.py:47
  1025.0 220.2 %reduce-scatter.17.cloned.1.call-start = ((), (), s32[]{:S(2)}) async-start(), calls=%async_computation.18 | async-start | bytes 15925248 | tf_op jit(solution)/shard_map/reduce_scatter | solution.py:47
  1048.5 322.9 %reduce-scatter.15.cloned.1.call-start = ((), (), s32[]{:S(2)}) async-start(), calls=%async_computation.17 | async-start | bytes 15925248 | tf_op jit(solution)/shard_map/reduce_scatter | solution.py:47
  1067.6 401.3 %reduce-scatter.11.cloned.1.call-start = ((), (), s32[]{:S(2)}) async-start(), calls=%async_computation.15 | async-start | bytes 11943936 | tf_op jit(solution)/shard_map/reduce_scatter | solution.py:47
  1112.4 782.8 %all-reduce.12.cloned.1.call-start = ((), (), s32[]{:S(2)}) async-start(), calls=%async_computation.19 | async-start | bytes 47775744 | tf_op jit(solution)/shard_map/psum | solution.py:239
  (46 other events, 516.5 us)
Sparse Core Ops, SparseCore 0:
  9.6 191.9 all-gather.10
  203.1 99.1 all-gather.12
  322.5 63.0 all-gather.16
  387.5 62.6 all-gather.14
  451.6 39.3 all-gather.18
  492.4 130.9 all-gather.20
  625.0 130.9 all-gather.22
  889.1 59.9 reduce-scatter.8
  1017.0 60.0 reduce-scatter.6
  1079.8 37.9 reduce-scatter.12
  1120.7 124.4 reduce-scatter.16
  1248.1 123.2 reduce-scatter.14
  1374.2 94.6 reduce-scatter.10
  1475.5 419.5 all-reduce.11
where the time goes:
time: 1940 us; the launch traced here: 1930 us
  waiting for transfers between devices  1190 us (61%)
  matrix products  381 us (20%)
  other arithmetic  150 us (8%)
  local copies, waits for them, and re-layouts  94.9 us (5%)
  blocking collectives  93.2 us (5%)
    psum x1, waiting for transfers between devices, shards(): lax.psum(pair_ada[0].astype(jnp.bfloat16), 'replica').astype(jnp.float32)  356 us
    reduce_scatter x4, waiting for transfers between devices, owner_grads(): lax.psum_scatter(lax.dot_general(columns, grads, (((0,), (0,)), ((), ()))...  300 us
    all_gather x1, waiting for transfers between devices, shards(): lax.all_gather(w_ada, 'shard', axis=0, tiled=True)  186 us
    all_gather x1, waiting for transfers between devices, shards(): lax.all_gather(w_fc1, 'shard', axis=0, tiled=True)  120 us
    all_gather x1, waiting for transfers between devices, shards(): lax.all_gather(w_fc2, 'shard', axis=0, tiled=True)  113 us
    all_gather x1, waiting for transfers between devices, shards(): lax.all_gather(w_qkv, 'shard', axis=0, tiled=True)  90.6 us
    dot_general x5, matrix products, contract_last(): lax.dot_general(left, right, (((1,), (1,)), ((), ())), preferred_element_...  80.5 us
    dot_general x5, matrix products, forward_product(): jnp.dot(inputs, whole_pair[0], preferred_element_type=jnp.float32)  66.9 us
  transfers between devices with their start and end apart: 14, of which 11 were waited for; matrix products, arithmetic and copies ran while one was open for 23% of the time, Pallas kernels for 0%

commit v1 on v0

--- a/solution.py
+++ b/solution.py
@@ -42,20 +42,51 @@
     return contract_last(grads, whole_pair[0])
 
 
-def owner_grads(inputs, grads, weight_rows, bias_terms):
-    columns = lax.slice_in_dim(inputs, 0, weight_rows * lax.axis_size("shard"), axis=1)
-    weight_grad = lax.psum_scatter(
-        lax.dot_general(
-            columns, grads, (((0,), (0,)), ((), ())), preferred_element_type=jnp.float32
-        ).astype(jnp.bfloat16),
-        "shard",
-        scatter_dimension=0,
-        tiled=True,
-    ).astype(jnp.float32)
-    bias_grad = lax.psum_scatter(
-        bias_terms.astype(jnp.bfloat16), "shard", scatter_dimension=0, tiled=True
-    ).astype(jnp.float32)
-    return (weight_grad, bias_grad)
+def swap_cores(values):
+    return lax.ppermute(values, "core", [(0, 1), (1, 0)])
+
+
+def join_cores(mine, axis):
+    theirs = swap_cores(mine)
+    first = lax.axis_index("core") == 0
+    return jnp.stack(
+        [jnp.where(first, mine, theirs), jnp.where(first, theirs, mine)], axis=axis
+    )
+
+
+def gather_rows(weight):
+    rows, columns = weight.shape
+    cores = lax.axis_size("core")
+    part = rows // cores
+    mine = lax.dynamic_slice_in_dim(weight, lax.axis_index("core") * part, part, 0)
+    pieces = lax.all_gather(mine, "shard", axis=0, tiled=False)
+    whole = join_cores(pieces, 1)
+    return whole.reshape(rows * lax.axis_size("shard"), columns)
+
+
+def weight_grad(inputs, grads, after):
+    n_shard, n_core = (lax.axis_size("shard"), lax.axis_size("core"))
+    terms = lax.dot_general(
+        inputs, grads, (((0,), (0,)), ((), ())), preferred_element_type=jnp.float32
+    ).astype(jnp.bfloat16)
+    rows, columns = terms.shape
+    part = rows // (n_shard * n_core)
+    terms = terms.reshape(n_shard, n_core, part, columns)
+    core = lax.axis_index("core")
+    keep = lax.dynamic_index_in_dim(terms, core, 1, keepdims=False)
+    send = lax.dynamic_index_in_dim(terms, 1 - core, 1, keepdims=False)
+    terms = (keep.astype(jnp.float32) + swap_cores(send).astype(jnp.float32)).astype(jnp.bfloat16)
+    terms = lax.psum_scatter(terms, "shard", scatter_dimension=0, tiled=True)
+    terms = terms.reshape(part, columns)
+    if after is not None:
+        terms, _ = lax.optimization_barrier((terms, after))
+    total = lax.psum(terms, "chip")
+    return total
+
+
+def finish_grad(total):
+    joined = join_cores(total, 0).astype(jnp.float32)
+    return joined.reshape(2 * total.shape[0], total.shape[1])
 
 
 def shards(
@@ -78,27 +109,26 @@
     n_rows = slots * block
     scale = 1.0 / math.sqrt(HDIM)
     live = (jnp.arange(slots, dtype=jnp.int32) < counts[0]).astype(jnp.float32)[:, None, None]
-    gathered = (
-        lax.all_gather(w_ada, "shard", axis=0, tiled=True),
-        lax.all_gather(b_ada, "shard", axis=0, tiled=True),
-        lax.all_gather(w_qkv, "shard", axis=0, tiled=True),
-        lax.all_gather(b_qv, "shard", axis=0, tiled=True),
-        lax.all_gather(w_proj, "shard", axis=0, tiled=True),
-        lax.all_gather(b_proj, "shard", axis=0, tiled=True),
-        lax.all_gather(w_fc1, "shard", axis=0, tiled=True),
-        lax.all_gather(b_fc1, "shard", axis=0, tiled=True),
-        lax.all_gather(w_fc2, "shard", axis=0, tiled=True),
-        lax.all_gather(b_fc2, "shard", axis=0, tiled=True),
-    )
-    full_ada = (gathered[0], gathered[1])
-    full_qkv = (gathered[2], gathered[3])
-    full_proj = (gathered[4], gathered[5])
-    full_fc1 = (gathered[6], gathered[7])
-    full_fc2 = (gathered[8], gathered[9])
+    index = lax.axis_index("shard")
+    biases = (b_ada, b_qv, b_proj, b_fc1, b_fc2)
+    bias_all = lax.all_gather(jnp.concatenate(biases), "shard", axis=0, tiled=False)
+    full_bias = []
+    start = 0
+    for bias in biases:
+        size = bias.shape[0]
+        full_bias.append(bias_all[:, start : start + size].reshape(-1))
+        start += size
+    full_qkv = (gather_rows(w_qkv), full_bias[1])
+    full_proj = (gather_rows(w_proj), full_bias[2])
+    full_fc1 = (gather_rows(w_fc1), full_bias[3])
+    full_fc2 = (gather_rows(w_fc2), full_bias[4])
     cond_float = conditions.astype(jnp.float32)
     cond_act = jax.nn.silu(cond_float).astype(jnp.bfloat16)
-    ada_prod, ada_bias = forward_product(cond_act, full_ada)
-    modul = ada_prod + ada_bias
+    ada_rows = w_ada.shape[0]
+    ada_length = b_ada.shape[0]
+    own_cond = lax.dynamic_slice_in_dim(cond_act, index * ada_rows, ada_rows, 1)
+    ada_part = jnp.dot(own_cond, w_ada, preferred_element_type=jnp.float32)
+    modul = lax.psum(ada_part, "shard") + full_bias[0].astype(jnp.float32)
     shift_a, scale_a, gate_a, shift_m, scale_m, gate_m = [
         piece[:, None, :] for piece in jnp.split(modul, 6, axis=1)
     ]
@@ -133,6 +163,7 @@
     attended = jnp.einsum(
         "shqk,skhd->sqhd", probs_low, values_h, preferred_element_type=jnp.float32
     )
+    attended_wide = attended
     attended = attended.astype(jnp.bfloat16).reshape(n_rows, width)
     proj_prod, proj_bias = forward_product(attended, full_proj)
     branch_a = (proj_prod + proj_bias).reshape(slots, block, width)
@@ -149,21 +180,20 @@
     d_out = cotangent.astype(jnp.float32) * live
     d_gate_m = jnp.sum(d_out * branch_m, axis=1)
     d_branch_m = (gate_m * d_out).astype(jnp.bfloat16).reshape(n_rows, width)
-    pair_fc2 = owner_grads(
-        hidden, d_branch_m, w_fc2.shape[0], jnp.sum(d_branch_m, axis=0, dtype=jnp.float32)
-    )
+    sum_fc2 = weight_grad(hidden, d_branch_m, None)
+    bias_fc2 = jnp.sum(d_branch_m, axis=0, dtype=jnp.float32)
     d_hidden = backward_product(d_branch_m, full_fc2)
     d_pre = gelu_back(d_hidden)[0].astype(jnp.bfloat16)
-    pair_fc1 = owner_grads(mixed, d_pre, w_fc1.shape[0], jnp.sum(d_pre, axis=0, dtype=jnp.float32))
+    sum_fc1 = weight_grad(mixed, d_pre, sum_fc2)
+    bias_fc1 = jnp.sum(d_pre, axis=0, dtype=jnp.float32)
     d_mixed = backward_product(d_pre, full_fc1).reshape(slots, block, width)
     d_shift_m = jnp.sum(d_mixed, axis=1)
     d_scale_m = jnp.sum(d_mixed * norm_m, axis=1)
     d_resid = d_out + layer_back(norm_m, inv_m, d_mixed * (1.0 + scale_m))
     d_gate_a = jnp.sum(d_resid * branch_a, axis=1)
     d_branch_a = (gate_a * d_resid).astype(jnp.bfloat16).reshape(n_rows, width)
-    pair_proj = owner_grads(
-        attended, d_branch_a, w_proj.shape[0], jnp.sum(d_branch_a, axis=0, dtype=jnp.float32)
-    )
+    sum_proj = weight_grad(attended, d_branch_a, sum_fc1)
+    bias_proj = jnp.sum(d_branch_a, axis=0, dtype=jnp.float32)
     d_attended = (
         backward_product(d_branch_a, full_proj)
         .astype(jnp.bfloat16)
@@ -176,7 +206,8 @@
     d_probs = jnp.einsum(
         "sqhd,skhd->shqk", d_attended, values_h, preferred_element_type=jnp.float32
     )
-    inner = jnp.sum(d_probs * probs, axis=-1, keepdims=True)
+    inner = jnp.sum(d_attended.astype(jnp.float32) * attended_wide, axis=-1)
+    inner = jnp.swapaxes(inner, 1, 2)[..., None]
     d_scores = (probs * (d_probs - inner)).astype(jnp.bfloat16)
     d_query = (
         (
@@ -212,7 +243,7 @@
     qv_terms = jnp.concatenate(
         [jnp.sum(d_query, axis=0, dtype=jnp.float32), jnp.sum(d_values, axis=0, dtype=jnp.float32)]
     )
-    pair_qkv = owner_grads(normed, d_qkv, w_qkv.shape[0], qv_terms)
+    sum_qkv = weight_grad(normed, d_qkv, sum_proj)
     d_normed = backward_product(d_qkv, full_qkv).reshape(slots, block, width)
     d_shift_a = jnp.sum(d_normed, axis=1)
     d_scale_a = jnp.sum(d_normed * norm_a, axis=1)
@@ -220,61 +251,58 @@
     d_modul_part = jnp.concatenate(
         [d_shift_a, d_scale_a, d_gate_a, d_shift_m, d_scale_m, d_gate_m], axis=1
     )
-    d_modul = lax.psum(d_modul_part.astype(jnp.bfloat16), "shard")
-    index = lax.axis_index("shard")
-    ada_rows = w_ada.shape[0]
-    ada_length = b_ada.shape[0]
-    own_cond = lax.dynamic_slice_in_dim(cond_act, index * ada_rows, ada_rows, 1)
+    d_modul = lax.psum(d_modul_part, "shard").astype(jnp.bfloat16)
+    cond_all = lax.all_gather(own_cond, ("chip", "core"), axis=0, tiled=True)
+    d_modul_all = lax.all_gather(d_modul, ("chip", "core"), axis=0, tiled=True)
     grad_w_ada = lax.dot_general(
-        own_cond, d_modul, (((0,), (0,)), ((), ())), preferred_element_type=jnp.float32
+        cond_all, d_modul_all, (((0,), (0,)), ((), ())), preferred_element_type=jnp.float32
     )
     grad_b_ada = lax.dynamic_slice_in_dim(
-        jnp.sum(d_modul, axis=0, dtype=jnp.float32), index * ada_length, ada_length, 0
-    )
-    pair_ada = (grad_w_ada, grad_b_ada)
-    d_cond_act = backward_product(d_modul, full_ada)
+        jnp.sum(d_modul_all, axis=0, dtype=jnp.float32), index * ada_length, ada_length, 0
+    )
+    d_cond_act = lax.all_gather(contract_last(d_modul, w_ada), "shard", axis=1, tiled=True)
     _, silu_back = jax.vjp(jax.nn.silu, cond_float)
     grad_conditions = silu_back(d_cond_act)[0]
-    summed = (
-        lax.psum(pair_ada[0].astype(jnp.bfloat16), "replica").astype(jnp.float32),
-        lax.psum(pair_ada[1].astype(jnp.bfloat16), "replica").astype(jnp.float32),
-        lax.psum(pair_qkv[0].astype(jnp.bfloat16), "replica").astype(jnp.float32),
-        lax.psum(pair_qkv[1].astype(jnp.bfloat16), "replica").astype(jnp.float32),
-        lax.psum(pair_proj[0].astype(jnp.bfloat16), "replica").astype(jnp.float32),
-        lax.psum(pair_proj[1].astype(jnp.bfloat16), "replica").astype(jnp.float32),
-        lax.psum(pair_fc1[0].astype(jnp.bfloat16), "replica").astype(jnp.float32),
-        lax.psum(pair_fc1[1].astype(jnp.bfloat16), "replica").astype(jnp.float32),
-        lax.psum(pair_fc2[0].astype(jnp.bfloat16), "replica").astype(jnp.float32),
-        lax.psum(pair_fc2[1].astype(jnp.bfloat16), "replica").astype(jnp.float32),
-    )
-    pair_ada = (summed[0], summed[1])
-    pair_qkv = (summed[2], summed[3])
-    pair_proj = (summed[4], summed[5])
-    pair_fc1 = (summed[6], summed[7])
-    pair_fc2 = (summed[8], summed[9])
+    bias_terms = lax.psum(
+        jnp.concatenate([qv_terms, bias_proj, bias_fc1, bias_fc2]), ("chip", "core", "shard")
+    )
+    bias_grads = []
+    start = 0
+    for bias in biases[1:]:
+        size = bias.shape[0]
+        bias_grads.append(
+            lax.dynamic_slice_in_dim(bias_terms, start + index * size, size, 0)
+        )
+        start += size * lax.axis_size("shard")
     return (
         output,
         grad_latents,
         grad_conditions,
-        pair_ada[0],
-        pair_ada[1],
-        pair_qkv[0],
-        pair_qkv[1],
-        pair_proj[0],
-        pair_proj[1],
-        pair_fc1[0],
-        pair_fc1[1],
-        pair_fc2[0],
-        pair_fc2[1],
+        grad_w_ada,
+        grad_b_ada,
+        finish_grad(sum_qkv),
+        bias_grads[0],
+        finish_grad(sum_proj),
+        bias_grads[1],
+        finish_grad(sum_fc1),
+        bias_grads[2],
+        finish_grad(sum_fc2),
+        bias_grads[3],
     )
 
 
 def solution(mesh):
+    names = mesh.axis_names
+    n_replica, n_shard = (mesh.shape["replica"], mesh.shape["shard"])
+    devices = mesh.devices.transpose(names.index("replica"), names.index("shard"))
+    fine = jax.sharding.Mesh(
+        devices.reshape(n_replica // 2, 2, n_shard), ("chip", "core", "shard")
+    )
     placed = (
-        P("replica", "shard", None),
-        P("replica", None),
-        P("replica", "shard", None),
-        P("replica"),
+        P(("chip", "core"), "shard", None),
+        P(("chip", "core"), None),
+        P(("chip", "core"), "shard", None),
+        P(("chip", "core")),
         P("shard", None),
         P("shard"),
         P("shard", None),
@@ -288,12 +316,12 @@
     )
     return jax.shard_map(
         shards,
-        mesh=mesh,
+        mesh=fine,
         in_specs=placed,
         out_specs=(
-            P("replica", "shard", None),
-            P("replica", "shard", None),
-            P("replica", None),
+            P(("chip", "core"), "shard", None),
+            P(("chip", "core"), "shard", None),
+            P(("chip", "core"), None),
             P("shard", None),
             P("shard"),
             P("shard", None),

time: 1940 us -> 1370 us (0.71)
  waiting for transfers between devices: 1190 us -> 574 us
  local copies, waits for them, and re-layouts: 94.9 us -> 125 us
  matrix products: 381 us -> 360 us
    all_gather x5 -> x4, waiting for transfers between devices: 510 us -> 152 us  [gather_rows(): pieces = lax.all_gather(mine, 'shard', axis=0, tiled=False)]
    reduce_scatter x4, waiting for transfers between devices: 300 us -> 90.6 us  [weight_grad(): terms = lax.psum_scatter(terms, 'shard', scatter_dimension=0, tiled=True)]
    psum x1 -> x4, waiting for transfers between devices: 356 us -> 289 us  [weight_grad(): total = lax.psum(terms, 'chip')]
    another operation x0 -> x16, other arithmetic: none -> 63.1 us  [join_cores(): jnp.stack([jnp.where(first, mine, theirs), jnp.where(first, theirs, mine)...]
    convert_element_type x12 -> x11, other arithmetic: 88.7 us -> 40.9 us  [the longest x4 21.7 us: weight_grad(): (keep.astype(jnp.float32) + swap_cores(send).astype(jnp.float32)).astype(...]
    all_gather x3 -> x4, blocking collectives: 14.4 us -> 53.7 us  [the longest x1 24.1 us: shards(): d_modul_all = lax.all_gather(d_modul, ('chip', 'core'), axis=0, tiled=True)]
    reduce_scatter x1, waiting for transfers between devices: 0.01 us -> 20.9 us  [shards(): lax.psum_scatter(value_terms.astype(jnp.bfloat16), 'shard', scatter_dimen...]
    psum x2 -> x3, blocking collectives: 73.7 us -> 55.5 us  [the longest x1 37.6 us: shards(): lax.psum(jnp.concatenate([qv_terms, bias_proj, bias_fc1, bias_fc2]), ('ch...]
  transfers between devices with their start and end apart: 14 -> 28, of which waited for: 11 -> 13; matrix products, arithmetic and copies ran while one was open for 23% -> 39% of each run, Pallas kernels for 0% -> 0%
where the time goes in v1:
time: 1370 us; the launch traced here: 1360 us
  waiting for transfers between devices  574 us (42%)
  matrix products  360 us (26%)
  other arithmetic  169 us (12%)
  local copies, waits for them, and re-layouts  125 us (9%)
  blocking collectives  109 us (8%)
  between operations  16.1 us (1%)
    psum x4, waiting for transfers between devices, weight_grad(): total = lax.psum(terms, 'chip')  289 us
    all_gather x4, waiting for transfers between devices, gather_rows(): pieces = lax.all_gather(mine, 'shard', axis=0, tiled=False)  152 us
    reduce_scatter x4, waiting for transfers between devices, weight_grad(): terms = lax.psum_scatter(terms, 'shard', scatter_dimension=0, tiled=True)  90.6 us
    dot_general x5, matrix products, contract_last(): lax.dot_general(left, right, (((1,), (1,)), ((), ())), preferred_element_...  78.1 us
    another operation x16, other arithmetic, join_cores(): jnp.stack([jnp.where(first, mine, theirs), jnp.where(first, theirs, mine)...  63.1 us
    dot_general x4, matrix products, weight_grad(): lax.dot_general(inputs, grads, (((0,), (0,)), ((), ())), preferred_elemen...  55.4 us
    dot_general x4, matrix products, forward_product(): jnp.dot(inputs, whole_pair[0], preferred_element_type=jnp.float32)  52.9 us
    dot_general x1, matrix products, shards(): jnp.einsum('sqhd,skhd->shqk', d_attended, values_h, preferred_element_typ...  40 us
  transfers between devices with their start and end apart: 28, of which 13 were waited for; matrix products, arithmetic and copies ran while one was open for 39% of the time, Pallas kernels for 0%

profile of v1, /device:TPU:0, one launch (start us, length us, event | category | flops | bytes accessed | tf_op | source)
XLA Modules:
  0.0 1356.4 jit_solution(5749713630772943146)
XLA Ops:
  24.4 43.2 %all-gather.20.cloned.1.call-done = bf16[576,3456]{1,0:T(8,128)(2,1)} async-done(((bf16[288,3456]{1,0:T(8,128)(2,1)}), bf16[576,3456]{1,0:T(8,128)(2,1)}) %all-gather.20.cloned.1.call-update) | async-done | bytes 3981328 | tf_op jit(solution)/shard_map/all_gather | solution.py:62
  91.4 48.1 %all-gather.26.cloned.1.call-done = bf16[2304,1152]{1,0:T(8,128)(2,1)} async-done(((bf16[1152,1152]{1,0:T(8,128)(2,1)}), bf16[2304,1152]{1,0:T(8,128)(2,1)}) %all-gather.26.cloned.1.call-update) | async-done | bytes 5308432 | tf_op jit(solution)/shard_map/all_gather | solution.py:62
  176.7 60.8 %all-gather.24.cloned.1.call-done = bf16[576,4608]{1,0:T(8,128)(2,1)} async-done(((bf16[288,4608]{1,0:T(8,128)(2,1)}), bf16[576,4608]{1,0:T(8,128)(2,1)}) %all-gather.24.cloned.1.call-update) | async-done | bytes 5308432 | tf_op jit(solution)/shard_map/all_gather | solution.py:62
  308.2 27.4 %multiply_reduce_fusion = (f32[2,16,512]{2,1,0:T(8,128)S(1)}, f32[2,16,512,1024]{3,2,1,0:T(8,128)}) fusion(bf16[2,512,16,72]{1,3,2,0:T(8,128)(2,1)} %copy.62, bf16[2,1024,16,72]{1,3,2,0:T(8,128)(2,1)} %bitcast.194), kind=kOutput, calls=%fused_computation.4 | convolution fusion | flops 2449457152 | bytes 74252288 | tf_op jit(solution)/shard_map/sqhd,skhd->shqk/dot_general | solution.py:158
  335.6 21.3 %exponential_reduce_fusion = f32[2,16,512]{2,1,0:T(8,128)S(1)} fusion(f32[2,16,512,1024]{3,2,1,0:T(8,128)} %get-tuple-element.71, f32[2,16,512]{2,1,0:T(8,128)S(1)} %get-tuple-element.70), kind=kLoop, calls=%fused_computation.2 | loop fusion | flops 50315264 | bytes 67239936 | tf_op jit(solution)/shard_map/reduce_sum | solution.py:161
  372.3 28.1 %bitcast_convert_fusion.2 = (bf16[2,512,16,72]{1,3,2,0:T(8,128)(2,1)}, f32[2,16,72,512]{3,2,1,0:T(8,128)}) fusion(bf16[2,1024,16,72]{1,3,2,0:T(8,128)(2,1)} %bitcast.192, f32[2,16,512,1024]{3,2,1,0:T(8,128)} %get-tuple-element.71, f32[2,16,512]{2,1,0:T(8,128)S(1)} %log_add_fusion), kind=kOutput, calls=%fused_computation.77 | convolution fusion | flops 2467430400 | bytes 78970880 | tf_op jit(solution)/shard_map/shqk,skhd->sqhd/dot_general | solution.py:163
  432.1 22.5 %convolution_convert_fusion = bf16[4608,1152]{1,0:T(8,128)(2,1)} fusion(bf16[1024,1152]{1,0:T(8,128)(2,1)S(1)} %bitcast.236, f32[1024,4608]{1,0:T(8,128)} %fusion.61, f32[4608]{0:T(1024)S(1)} %reshape.282), kind=kOutput, calls=%fused_computation.7 | convolution fusion | flops 10924130304 | bytes 31868928 | tf_op jit(solution)/shard_map/dot_general | solution.py:69
  459.9 29.6 %convert_reduce_fusion = (f32[4608]{0:T(1024)}, bf16[1024,4608]{1,0:T(8,128)(2,1)}) fusion(f32[1024,4608]{1,0:T(8,128)} %fusion.61, f32[4608]{0:T(1024)S(1)} %reshape.282, bf16[1024,1152]{1,0:T(8,128)(2,1)S(1)} %bitcast.237, bf16[4608,1152]{1,0:T(8,128)(2,1)} %bitcast.205), kind=kOutput, calls=%fused_computation.16 | convolution fusion | flops 10980159488 | bytes 41324544 | tf_op jit(solution)/shard_map/dot_general | solution.py:29
  489.4 21.3 %multiply_reduce_fusion.2 = (f32[2,1152]{1,0:T(2,128)}, f32[2,512]{1,0:T(2,128)S(1)}, f32[2,512]{1,0:T(2,128)S(1)}, f32[2,1152]{1,0:T(2,128)}, f32[2,512,1152]{2,1,0:T(8,128)}) fusion(f32[2,512,1152]{2,1,0:T(8,128)} %copy-done.2, f32[2,512]{1,0:T(2,128)S(1)} %add_rsqrt_fusion, f32[2,512]{1,0:T(2,128)S(1)} %broadcast_multiply_fusion.4, ...), kind=kOutput, calls=%fused_computation.84 | convolution fusion | flops 10882246656 | bytes 29535232 | tf_op jit(solution)/shard_map/dot_general | solution.py:29
  519.2 21.6 %convolution_add_fusion = f32[1024,1152]{1,0:T(8,128)S(1)} fusion(bf16[4608,1152]{1,0:T(8,128)(2,1)} %bitcast.206, f32[1152]{0:T(1024)S(1)} %copy-done.47, f32[1024,4608]{1,0:T(8,128)} %fusion.61, f32[4608]{0:T(1024)S(1)} %reshape.282), kind=kOutput, calls=%fused_computation.62 | convolution fusion | flops 10920001536 | bytes 34232832 | tf_op jit(solution)/shard_map/dot_general | solution.py:36
  576.8 40.0 %multiply_convert_fusion = bf16[2,16,512,1024]{3,2,1,0:T(8,128)(2,1)} fusion(f32[2,16,512,1024]{3,2,1,0:T(8,128)} %get-tuple-element.71, f32[2,16,512]{2,1,0:T(8,128)S(1)} %bitcast.247, f32[2,16,512]{2,1,0:T(8,128)S(1)} %copy-done.12, bf16[2,512,16,72]{1,3,2,0:T(8,128)(2,1)S(1)} %copy-done.5, bf16[2,1024,16,72]{1,3,2,0:T(8,128)(2,1)} %bitcast.193), kind=kOutput, calls=%fused_computation | convolution fusion | flops 2499805184 | bytes 107872256 | tf_op jit(solution)/shard_map/sqhd,skhd->shqk/dot_general | solution.py:206
  616.9 19.4 %multiply_convert_fusion.2 = bf16[2,16,72,1024]{3,2,1,0:T(8,128)(2,1)} fusion(bf16[2,512,16,72]{1,3,2,0:T(8,128)(2,1)} %copy.62, bf16[2,16,512,1024]{3,2,1,0:T(8,128)(2,1)} %multiply_convert_fusion), kind=kOutput, calls=%fused_computation.25 | convolution fusion | flops 2420637696 | bytes 40632320 | tf_op jit(solution)/shard_map/shqk,sqhd->skhd/dot_general | solution.py:221
  643.1 27.6 %fusion.43 = bf16[2,16,72,1024]{3,2,1,0:T(8,128)(2,1)} fusion(bf16[2,512,16,72]{1,3,2,0:T(8,128)(2,1)} %copy.68, f32[2,16,512,1024]{3,2,1,0:T(8,128)} %get-tuple-element.71, f32[2,16,512]{2,1,0:T(8,128)S(1)} %copy-done.12), kind=kOutput, calls=%fused_computation.105 | convolution fusion | flops 2468610048 | bytes 74252288 | tf_op jit(solution)/shard_map/shqk,sqhd->skhd/dot_general | solution.py:226
  716.4 18.0 %convert_reduce_fusion.5 = (f32[16,72]{1,0:T(8,128)S(1)}, bf16[2,16,72,512]{3,2,1,0:T(8,128)(2,1)S(1)}) fusion(bf16[2,1024,16,72]{1,3,2,0:T(8,128)(2,1)} %bitcast.195, bf16[2,16,512,1024]{3,2,1,0:T(8,128)(2,1)} %multiply_convert_fusion), kind=kOutput, calls=%fused_computation.82 | convolution fusion | flops 2420636672 | bytes 40636928 | tf_op jit(solution)/shard_map/shqk,skhd->sqhd/dot_general | solution.py:214
  744.8 20.9 %reduce-scatter.9.cloned.1.call-done = bf16[2,512,1152]{2,1,0:T(8,128)(2,1)} async-done(((bf16[2,1024,1152]{2,1,0:T(8,128)(2,1)}), bf16[2,512,1152]{2,1,0:T(8,128)(2,1)}) %reduce-scatter.9.cloned.1.call-update) | async-done | bytes 2359312 | tf_op jit(solution)/shard_map/reduce_scatter | solution.py:236
  787.6 47.2 %reduce-scatter.15.cloned.1.call-done = bf16[1,288,4608]{2,1,0:T(8,128)(2,1)} async-done(((bf16[2,288,4608]{2,1,0:T(8,128)(2,1)}), bf16[1,288,4608]{2,1,0:T(8,128)(2,1)}) %reduce-scatter.15.cloned.1.call-update) | async-done | bytes 2654224 | tf_op jit(solution)/shard_map/reduce_scatter | solution.py:79
  834.8 119.8 %all-reduce.5.cloned.1.call-done = bf16[1152,1152]{1,0:T(8,128)(2,1)} async-done(((bf16[1152,1152]{1,0:T(8,128)(2,1)}), bf16[1152,1152]{1,0:T(8,128)(2,1)}) %all-reduce.5.cloned.1.call-update) | async-done | bytes 2654224 | tf_op jit(solution)/shard_map/psum | solution.py:83
  954.7 19.7 %all-gather.7 = bf16[16,2,576]{2,1,0:T(2,128)(2,1)S(1)} all-gather(bf16[1,2,576]{2,1,0:T(2,128)(2,1)S(1)} %bitcast.254), channel_id=1, replica_groups=mesh['chip'=8,'core'=2,'shard'=2] {'chip','core'}, dimensions={0}, use_global_device_ids=true | all-gather | bytes 39168 | tf_op jit(solution)/shard_map/all_gather | solution.py:255
  987.3 17.0 %fusion.38 = (f32[2,1152]{1,0:T(2,128)S(1)}, f32[2,512]{1,0:T(2,128)S(1)}, f32[2,512]{1,0:T(2,128)S(1)}, f32[2,1152]{1,0:T(2,128)S(1)}, f32[2,512,1152]{2,1,0:T(8,128)}) fusion(bf16[2,512,1152]{2,1,0:T(8,128)(2,1)} %param.14, f32[2,512]{1,0:T(2,128)S(1)} %copy-done.38, f32[2,512]{1,0:T(2,128)S(1)} %copy-done.32, f32[2,1152]{1,0:T(2,128)S(1)} %copy-done.30, ...), kind=kOutput, calls=%fused_computation.69 | convolution fusion | flops 8186750976 | bytes 22162432 | tf_op jit(solution)/shard_map/dot_general | solution.py:29
  1012.8 37.6 %psum.55 = f32[9216]{0:T(1024)S(1)} all-reduce(f32[9216]{0:T(1024)S(1)} %constant_dynamic-update-slice_fusion.10), channel_id=1, replica_groups=mesh['chip'=8,'core'=2,'shard'=2] {'chip','core','shard'}, use_global_device_ids=true, to_apply=%region_35.36 | all-reduce | flops 9216 | bytes 73728 | tf_op jit(solution)/shard_map/psum | solution.py:266
  1071.5 24.1 %all-gather.8 = bf16[16,2,6912]{2,1,0:T(2,128)(2,1)S(1)} all-gather(bf16[1,2,6912]{2,1,0:T(2,128)(2,1)S(1)} %bitcast.249), channel_id=1, replica_groups=mesh['chip'=8,'core'=2,'shard'=2] {'chip','core'}, dimensions={0}, use_global_device_ids=true | all-gather | bytes 470016 | tf_op jit(solution)/shard_map/all_gather | solution.py:256
  1112.7 43.4 %reduce-scatter.11.cloned.1.call-done = bf16[1,288,3456]{2,1,0:T(8,128)(2,1)} async-done(((bf16[2,288,3456]{2,1,0:T(8,128)(2,1)}), bf16[1,288,3456]{2,1,0:T(8,128)(2,1)}) %reduce-scatter.11.cloned.1.call-update) | async-done | bytes 1990672 | tf_op jit(solution)/shard_map/reduce_scatter | solution.py:79
  1156.1 77.1 %all-reduce.9.cloned.1.call-done = bf16[288,1152]{1,0:T(8,128)(2,1)} async-done(((bf16[288,1152]{1,0:T(8,128)(2,1)}), bf16[288,1152]{1,0:T(8,128)(2,1)}) %all-reduce.9.cloned.1.call-update) | async-done | bytes 663568 | tf_op jit(solution)/shard_map/psum | solution.py:83
  1242.7 92.6 %all-reduce.11.cloned.1.call-done = bf16[288,3456]{1,0:T(8,128)(2,1)} async-done(((bf16[288,3456]{1,0:T(8,128)(2,1)}), bf16[288,3456]{1,0:T(8,128)(2,1)}) %all-reduce.11.cloned.1.call-update) | async-done | bytes 1990672 | tf_op jit(solution)/shard_map/psum | solution.py:83
  (301 shorter events, 412.0 us)
Async XLA Ops:
  7.2 60.3 %all-gather.20.cloned.1.call-start = ((), (), s32[]{:S(2)}) async-start(), calls=%async_computation.18 | async-start | bytes 5971968 | tf_op jit(solution)/shard_map/all_gather | solution.py:62
  10.3 129.2 %all-gather.26.cloned.1.call-start = ((), (), s32[]{:S(2)}) async-start(), calls=%async_computation.21 | async-start | bytes 7962624 | tf_op jit(solution)/shard_map/all_gather | solution.py:62
  14.0 156.8 %all-gather.22.cloned.1.call-start = ((), (), s32[]{:S(2)}) async-start(), calls=%async_computation.19 | async-start | bytes 1990656 | tf_op jit(solution)/shard_map/all_gather | solution.py:62
  14.9 222.5 %all-gather.24.cloned.1.call-start = ((), (), s32[]{:S(2)}) async-start(), calls=%async_computation.20 | async-start | bytes 7962624 | tf_op jit(solution)/shard_map/all_gather | solution.py:62
  18.4 283.1 %all-gather.18.cloned.1.call-start = ((), (), s32[]{:S(2)}) async-start(), calls=%async_computation.7 | async-start | bytes 7077888 | tf_op jit(solution)/shard_map/all_gather | solution.py:151
  67.5 72.0 %collective-permute-start = (bf16[2,288,3456]{2,1,0:T(8,128)(2,1)}, bf16[2,288,3456]{2,1,0:T(8,128)(2,1)}, u32[]{:S(2)}, u32[]{:S(2)}) collective-permute-start(bf16[2,288,3456]{2,1,0:T(8,128)(2,1)} %bitcast.224), channel_id=1, source_target_pairs={{0,2},{2,0},{1,3},{3,1},{4,6},{6,4},{5,7},{7,5},{8,10},{10,8},{9,1... | collective-permute-start | bytes 11943944 | tf_op jit(solution)/shard_map/ppermute | solution.py:46
  139.6 123.4 %collective-permute-start.3 = (bf16[2,1152,1152]{2,1,0:T(8,128)(2,1)}, bf16[2,1152,1152]{2,1,0:T(8,128)(2,1)}, u32[]{:S(2)}, u32[]{:S(2)}) collective-permute-start(bf16[2,1152,1152]{2,1,0:T(8,128)(2,1)} %bitcast.220), channel_id=1, source_target_pairs={{0,2},{2,0},{1,3},{3,1},{4,6},{6,4},{5,7},{7,5},{8,10},{10,8},{9,1... | collective-permute-start | bytes 15925256 | tf_op jit(solution)/shard_map/ppermute | solution.py:46
  170.2 195.4 %all-gather.16.cloned.1.call-start = ((), (), s32[]{:S(2)}) async-start(), calls=%async_computation.6 | async-start | bytes 7077888 | tf_op jit(solution)/shard_map/all_gather | solution.py:152
  237.5 44.6 %collective-permute-start.2 = (bf16[2,288,4608]{2,1,0:T(8,128)(2,1)}, bf16[2,288,4608]{2,1,0:T(8,128)(2,1)}, u32[]{:S(2)}, u32[]{:S(2)}) collective-permute-start(bf16[2,288,4608]{2,1,0:T(8,128)(2,1)} %bitcast.222), channel_id=1, source_target_pairs={{0,2},{2,0},{1,3},{3,1},{4,6},{6,4},{5,7},{7,5},{8,10},{10,8},{9,1... | collective-permute-start | bytes 15925256 | tf_op jit(solution)/shard_map/ppermute | solution.py:46
  262.9 453.5 %reduce-scatter.17.cloned.1.call-start = ((), (), s32[]{:S(2)}) async-start(), calls=%async_computation.13 | async-start | bytes 7962624 | tf_op jit(solution)/shard_map/reduce_scatter | solution.py:79
  459.9 50.9 %collective-permute-start.7 = (bf16[2,1152,1152]{2,1,0:T(8,128)(2,1)}, bf16[2,1152,1152]{2,1,0:T(8,128)(2,1)}, u32[]{:S(2)}, u32[]{:S(2)}) collective-permute-start(bf16[2,1152,1152]{2,1,0:T(8,128)(2,1)} %dynamic-slice_bitcast_fusion), channel_id=1, source_target_pairs={{0,2},{2,0},{1,3},{3,1},{4,6},{6,4},{5,7},{7,5},{8,10},{10,8},{9,1... | collective-permute-start | bytes 15925256 | tf_op jit(solution)/shard_map/ppermute | solution.py:46
  518.5 221.9 %reduce-scatter.7.cloned.1.call-start = ((), (), s32[]{:S(2)}) async-start(), calls=%async_computation.8 | async-start | bytes 7077888 | tf_op jit(solution)/shard_map/reduce_scatter | solution.py:233
  643.1 122.6 %reduce-scatter.9.cloned.1.call-start = ((), (), s32[]{:S(2)}) async-start(), calls=%async_computation.9 | async-start | bytes 7077888 | tf_op jit(solution)/shard_map/reduce_scatter | solution.py:236
  677.6 157.2 %reduce-scatter.15.cloned.1.call-start = ((), (), s32[]{:S(2)}) async-start(), calls=%async_computation.12 | async-start | bytes 7962624 | tf_op jit(solution)/shard_map/reduce_scatter | solution.py:79
  708.7 245.9 %all-reduce.5.cloned.1.call-start = ((), (), s32[]{:S(2)}) async-start(), calls=%async_computation.14 | async-start | bytes 5308416 | tf_op jit(solution)/shard_map/psum | solution.py:83
  715.9 23.0 %collective-permute-start.5 = (bf16[2,288,1152]{2,1,0:T(8,128)(2,1)S(1)}, bf16[2,288,1152]{2,1,0:T(8,128)(2,1)S(1)}, u32[]{:S(2)}, u32[]{:S(2)}) collective-permute-start(bf16[2,288,1152]{2,1,0:T(8,128)(2,1)S(1)} %dynamic-slice_bitcast_fusion.3), channel_id=1, source_target_pairs={{0,2},{2,0},{1,3},{3,1},{4,6},{6,4},{5,7},{7,5},{8,10},{10,8},{9,1... | collective-permute-start | bytes 3981320 | tf_op jit(solution)/shard_map/ppermute | solution.py:46
  716.3 389.7 %reduce-scatter.13.cloned.1.call-start = ((), (), s32[]{:S(2)}) async-start(), calls=%async_computation.11 | async-start | bytes 1990656 | tf_op jit(solution)/shard_map/reduce_scatter | solution.py:79
  740.4 365.6 %all-reduce.7.cloned.1.call-start = ((), (), s32[]{:S(2)}) async-start(), calls=%async_computation.15 | async-start | bytes 5308416 | tf_op jit(solution)/shard_map/psum | solution.py:83
  787.6 191.2 %collective-permute-start.4 = (bf16[2,288,3456]{2,1,0:T(8,128)(2,1)}, bf16[2,288,3456]{2,1,0:T(8,128)(2,1)}, u32[]{:S(2)}, u32[]{:S(2)}) collective-permute-start(bf16[2,288,3456]{2,1,0:T(8,128)(2,1)} %dynamic-slice_bitcast_fusion.2), channel_id=1, source_target_pairs={{0,2},{2,0},{1,3},{3,1},{4,6},{6,4},{5,7},{7,5},{8,10},{10,8},{9,1... | collective-permute-start | bytes 11943944 | tf_op jit(solution)/shard_map/ppermute | solution.py:46
  954.6 201.5 %reduce-scatter.11.cloned.1.call-start = ((), (), s32[]{:S(2)}) async-start(), calls=%async_computation.10 | async-start | bytes 5971968 | tf_op jit(solution)/shard_map/reduce_scatter | solution.py:79
  985.1 248.0 %all-reduce.9.cloned.1.call-start = ((), (), s32[]{:S(2)}) async-start(), calls=%async_computation.16 | async-start | bytes 1327104 | tf_op jit(solution)/shard_map/psum | solution.py:83
  1012.3 94.4 %collective-permute-start.11 = (bf16[1152,1152]{1,0:T(8,128)(2,1)}, bf16[1152,1152]{1,0:T(8,128)(2,1)}, u32[]{:S(2)}, u32[]{:S(2)}) collective-permute-start(bf16[1152,1152]{1,0:T(8,128)(2,1)} %all-reduce.5.cloned.1.call-done), channel_id=1, source_target_pairs={{0,2},{2,0},{1,3},{3,1},{4,6},{6,4},{5,7},{7,5},{8,10},{10,8},{9,1... | collective-permute-start | bytes 7962632 | tf_op jit(solution)/shard_map/ppermute | solution.py:46
  1106.0 229.2 %all-reduce.11.cloned.1.call-start = ((), (), s32[]{:S(2)}) async-start(), calls=%async_computation.17 | async-start | bytes 3981312 | tf_op jit(solution)/shard_map/psum | solution.py:83
  1106.3 228.9 %collective-permute-start.10 = (bf16[288,4608]{1,0:T(8,128)(2,1)}, bf16[288,4608]{1,0:T(8,128)(2,1)}, u32[]{:S(2)}, u32[]{:S(2)}) collective-permute-start(bf16[288,4608]{1,0:T(8,128)(2,1)} %all-reduce.7.cloned.1.call-done), channel_id=1, source_target_pairs={{0,2},{2,0},{1,3},{3,1},{4,6},{6,4},{5,7},{7,5},{8,10},{10,8},{9,1... | collective-permute-start | bytes 7962632 | tf_op jit(solution)/shard_map/ppermute | solution.py:46
  (61 other events, 1048.2 us)
Sparse Core Ops, SparseCore 0:
  10.5 57.0 all-gather.19
  69.7 69.8 all-gather.25
  141.7 24.4 all-gather.21
  168.1 69.2 all-gather.23
  238.9 62.6 all-gather.17
  302.9 62.6 all-gather.15
  518.6 66.5 reduce-scatter.16
  643.2 59.9 reduce-scatter.6
  705.6 59.9 reduce-scatter.8
  768.4 66.3 reduce-scatter.14
  838.5 116.0 all-reduce.4
  956.7 22.4 reduce-scatter.12
  983.2 118.2 all-reduce.6
  1104.3 51.6 reduce-scatter.10
  1159.7 73.3 all-reduce.8
  1236.6 98.6 all-reduce.10
